TPU v7x, 128 devices: a whole 4x4x4 slice. The times are simulated.
128 devices in a mesh: rep: 4 (over y_hi, core), fsdp: 32 (over z, y_lo, x).
Axes of the slice: x: 4, y: 4 (y_hi: 2, y_lo: 2; y = y_hi * 2 + y_lo), z: 4, core: 2. Of those that a mesh axis runs over, the one named last changes fastest.
Arguments:
- tokens: bfloat16 [16384, 1088], P(('rep', 'fsdp')), may hold values from -6 to 6
- segments: int32 [16384], P(('rep', 'fsdp')), may hold values from 0 to 101, as said below
- ln_gain: bfloat16 [1, 2, 1088], P(None, None, 'fsdp'), may hold values from 0.099609375 to 1.8984375
- ln_bias: bfloat16 [1, 2, 1088], P(None, None, 'fsdp'), may hold values from -1.75 to 1.75
- w_qkv: bfloat16 [1, 1088, 3264], P(None, 'fsdp'), may hold values from -1 to 1
- w_out: bfloat16 [1, 1088, 1088], P(None, 'fsdp'), may hold values from -0.5 to 0.5
- w_fc1: bfloat16 [1, 1088, 4352], P(None, 'fsdp'), may hold values from -0.1875 to 0.1875
- w_fc2: bfloat16 [1, 4352, 1088], P(None, 'fsdp'), may hold values from -0.09375 to 0.09375
- cotangent: bfloat16 [16384, 1088], P(('rep', 'fsdp')), may hold values from -6 to 6
Outputs:
- block_output: bfloat16 [16384, 1088], P(('rep', 'fsdp'))
- grad_tokens: float32 [16384, 1088], P(('rep', 'fsdp'))
- grad_ln_gain: float32 [1, 2, 1088], P(None, None, 'fsdp')
- grad_ln_bias: float32 [1, 2, 1088], P(None, None, 'fsdp')
- grad_qkv: float32 [1, 1088, 3264], P(None, 'fsdp')
- grad_out: float32 [1, 1088, 1088], P(None, 'fsdp')
- grad_fc1: float32 [1, 1088, 4352], P(None, 'fsdp')
- grad_fc2: float32 [1, 4352, 1088], P(None, 'fsdp')
Inputs may be any that keep to these rules, and one draw needn't show every extreme that they name: `segments`: segment numbers never fall along the token stream and each number from 0 to the most is used; a document is a run of equal numbers, 20 to 300 tokens long before sequence ends cut it.
All inputs are finite; a program needn't handle non-finite values.
Results may differ from a plain program's by a relative error of at most 0.025.
Values may be sent and summed in bfloat16 or wider, within the bound.
A program may use at most 192 MiB of HBM per device.

v0:
```python
import jax
import jax.numpy as jnp
from jax import lax
from jax.sharding import PartitionSpec as P

D = 1088
HEADS = 17
HEAD_DIM = 64
SEQ = 128
LAYERS = 1
EPS = 1e-05


def normalize(resid_in, gain_full, bias_full):
    feat_mean = jnp.mean(resid_in, axis=-1, keepdims=True)
    centred = resid_in - feat_mean
    feat_var = jnp.mean(centred * centred, axis=-1, keepdims=True)
    return centred * lax.rsqrt(feat_var + EPS) * gain_full + bias_full


def cross_rows(left_op, right_op):
    return lax.dot_general(
        left_op, right_op, (((0,), (0,)), ((), ())), preferred_element_type=jnp.float32
    )


def against(left_op, right_op):
    return lax.dot_general(
        left_op, right_op, (((1,), (1,)), ((), ())), preferred_element_type=jnp.float32
    )


def product(pattern, left_op, right_op):
    return jnp.einsum(pattern, left_op, right_op, preferred_element_type=jnp.float32)


def allowed_mask(seg_block):
    positions = jnp.arange(seg_block.shape[1])
    causal = positions[:, None] >= positions[None, :]
    same_doc = seg_block[:, :, None] == seg_block[:, None, :]
    return (causal[None] & same_doc)[:, None]


def scores_of(query_part, key_part, allowed):
    scores = product("sqhe,skhe->shqk", query_part, key_part) * 0.125
    return jnp.where(allowed, scores, -1e30)


def forward_layer(resid_in, allowed, whole_set):
    gain, bias, w_query, w_proj, w_first, w_second = whole_set
    row_count = resid_in.shape[0]
    seq_count = row_count // SEQ
    gain_full = gain.astype(jnp.float32)
    bias_full = bias.astype(jnp.float32)
    normed_one = normalize(resid_in, gain_full[0], bias_full[0]).astype(jnp.bfloat16)
    proj_qkv = jnp.dot(normed_one, w_query, preferred_element_type=jnp.float32).astype(jnp.bfloat16)
    proj_qkv = proj_qkv.reshape(seq_count, SEQ, 3, HEADS, HEAD_DIM)
    scores = scores_of(proj_qkv[:, :, 0], proj_qkv[:, :, 1], allowed)
    row_max = jnp.max(scores, axis=-1, keepdims=True)
    log_total = row_max + jnp.log(jnp.sum(jnp.exp(scores - row_max), axis=-1, keepdims=True))
    probs_half = jnp.exp(scores - log_total).astype(jnp.bfloat16)
    heads_out = (
        product("shqk,skhe->sqhe", probs_half, proj_qkv[:, :, 2])
        .astype(jnp.bfloat16)
        .reshape(row_count, D)
    )
    resid_mid = resid_in + jnp.dot(heads_out, w_proj, preferred_element_type=jnp.float32)
    normed_two = normalize(resid_mid, gain_full[1], bias_full[1]).astype(jnp.bfloat16)
    pre_act = jnp.dot(normed_two, w_first, preferred_element_type=jnp.float32)
    activated = jax.nn.gelu(pre_act, approximate=False).astype(jnp.bfloat16)
    resid_out = resid_mid + jnp.dot(activated, w_second, preferred_element_type=jnp.float32)
    return (
        resid_out,
        (
            resid_in,
            normed_one,
            proj_qkv,
            heads_out,
            log_total,
            resid_mid,
            normed_two,
            pre_act,
            activated,
        ),
    )


def backward_layer(grad_stream, kept_acts, allowed, whole_set):
    gain, bias, w_query, w_proj, w_first, w_second = whole_set
    (
        resid_in,
        normed_one,
        proj_qkv,
        heads_out,
        log_total,
        resid_mid,
        normed_two,
        pre_act,
        activated,
    ) = kept_acts
    row_count = grad_stream.shape[0]
    seq_count = row_count // SEQ
    gain_full = gain.astype(jnp.float32)
    bias_full = bias.astype(jnp.float32)
    grad_half = grad_stream.astype(jnp.bfloat16)
    grad_second = cross_rows(activated, grad_half)
    d_activated = against(grad_half, w_second)
    d_preact = jax.vjp(lambda inner_val: jax.nn.gelu(inner_val, approximate=False), pre_act)[1](
        d_activated
    )[0]
    d_preact = d_preact.astype(jnp.bfloat16)
    grad_first = cross_rows(normed_two, d_preact)
    d_normed_two = against(d_preact, w_first)
    pullback = jax.vjp(normalize, resid_mid, gain_full[1], bias_full[1])[1]
    d_mid_norm, d_gain_two, d_bias_two = pullback(d_normed_two)
    d_mid = grad_stream + d_mid_norm
    d_mid_half = d_mid.astype(jnp.bfloat16)
    grad_proj = cross_rows(heads_out, d_mid_half)
    d_heads = (
        against(d_mid_half, w_proj).astype(jnp.bfloat16).reshape(seq_count, SEQ, HEADS, HEAD_DIM)
    )
    query_part = proj_qkv[:, :, 0]
    key_part = proj_qkv[:, :, 1]
    value_part = proj_qkv[:, :, 2]
    scores = scores_of(query_part, key_part, allowed)
    probs_full = jnp.exp(scores - log_total)
    probs_half = probs_full.astype(jnp.bfloat16)
    d_value = product("shqk,sqhe->skhe", probs_half, d_heads)
    d_probs = product("sqhe,skhe->shqk", d_heads, value_part)
    heads_four = heads_out.reshape(seq_count, SEQ, HEADS, HEAD_DIM)
    row_delta = jnp.sum(d_heads.astype(jnp.float32) * heads_four.astype(jnp.float32), axis=-1)
    row_delta = jnp.transpose(row_delta, (0, 2, 1))[..., None]
    d_scores = (probs_full * (d_probs - row_delta) * 0.125).astype(jnp.bfloat16)
    d_query = product("shqk,skhe->sqhe", d_scores, key_part)
    d_key = product("shqk,sqhe->skhe", d_scores, query_part)
    d_qkv = (
        jnp.stack([d_query, d_key, d_value], axis=2).reshape(row_count, 3 * D).astype(jnp.bfloat16)
    )
    grad_query = cross_rows(normed_one, d_qkv)
    d_normed_one = against(d_qkv, w_query)
    pullback = jax.vjp(normalize, resid_in, gain_full[0], bias_full[0])[1]
    d_in_norm, d_gain_one, d_bias_one = pullback(d_normed_one)
    d_input = d_mid + d_in_norm
    grad_terms = (
        jnp.stack([d_gain_one, d_gain_two]),
        jnp.stack([d_bias_one, d_bias_two]),
        grad_query,
        grad_proj,
        grad_first,
        grad_second,
    )
    return (d_input, grad_terms)


def body(tokens, segments, ln_gain, ln_bias, w_qkv, w_out, w_fc1, w_fc2, cotangent):
    row_count = tokens.shape[0]
    allowed = allowed_mask(segments.reshape(row_count // SEQ, SEQ))
    stream = tokens.astype(jnp.float32)
    layer_idx = 0
    whole_set = (
        lax.all_gather(ln_gain[layer_idx], "fsdp", axis=1, tiled=True),
        lax.all_gather(ln_bias[layer_idx], "fsdp", axis=1, tiled=True),
        lax.all_gather(w_qkv[layer_idx], "fsdp", axis=0, tiled=True),
        lax.all_gather(w_out[layer_idx], "fsdp", axis=0, tiled=True),
        lax.all_gather(w_fc1[layer_idx], "fsdp", axis=0, tiled=True),
        lax.all_gather(w_fc2[layer_idx], "fsdp", axis=0, tiled=True),
    )
    stream, kept_acts = forward_layer(stream, allowed, whole_set)
    stored = [kept_acts]
    fetched = [whole_set]
    block_output = stream.astype(jnp.bfloat16)
    grad_stream = cotangent.astype(jnp.float32)
    shares = [None] * LAYERS
    for layer_idx in reversed(range(LAYERS)):
        whole_set = fetched[layer_idx]
        grad_stream, grad_terms = backward_layer(grad_stream, stored[layer_idx], allowed, whole_set)
        summed_part = (
            lax.psum_scatter(
                grad_terms[0].astype(jnp.bfloat16), "fsdp", scatter_dimension=1, tiled=True
            ).astype(jnp.float32),
            lax.psum_scatter(
                grad_terms[1].astype(jnp.bfloat16), "fsdp", scatter_dimension=1, tiled=True
            ).astype(jnp.float32),
            lax.psum_scatter(
                grad_terms[2].astype(jnp.bfloat16), "fsdp", scatter_dimension=0, tiled=True
            ).astype(jnp.float32),
            lax.psum_scatter(
                grad_terms[3].astype(jnp.bfloat16), "fsdp", scatter_dimension=0, tiled=True
            ).astype(jnp.float32),
            lax.psum_scatter(
                grad_terms[4].astype(jnp.bfloat16), "fsdp", scatter_dimension=0, tiled=True
            ).astype(jnp.float32),
            lax.psum_scatter(
                grad_terms[5].astype(jnp.bfloat16), "fsdp", scatter_dimension=0, tiled=True
            ).astype(jnp.float32),
        )
        column_sums = (
            lax.psum_scatter(
                summed_part[2].astype(jnp.bfloat16), "rep", scatter_dimension=1, tiled=True
            ).astype(jnp.float32),
            lax.psum_scatter(
                summed_part[3].astype(jnp.bfloat16), "rep", scatter_dimension=1, tiled=True
            ).astype(jnp.float32),
            lax.psum_scatter(
                summed_part[4].astype(jnp.bfloat16), "rep", scatter_dimension=1, tiled=True
            ).astype(jnp.float32),
            lax.psum_scatter(
                summed_part[5].astype(jnp.bfloat16), "rep", scatter_dimension=1, tiled=True
            ).astype(jnp.float32),
        )
        joined = (
            lax.all_gather(column_sums[0].astype(jnp.bfloat16), "rep", axis=1, tiled=True).astype(
                jnp.float32
            ),
            lax.all_gather(column_sums[1].astype(jnp.bfloat16), "rep", axis=1, tiled=True).astype(
                jnp.float32
            ),
            lax.all_gather(column_sums[2].astype(jnp.bfloat16), "rep", axis=1, tiled=True).astype(
                jnp.float32
            ),
            lax.all_gather(column_sums[3].astype(jnp.bfloat16), "rep", axis=1, tiled=True).astype(
                jnp.float32
            ),
        )
        norm_terms = lax.psum((summed_part[0], summed_part[1]), "rep")
        summed_part = (norm_terms[0], norm_terms[1], joined[0], joined[1], joined[2], joined[3])
        shares[layer_idx] = summed_part
    stacked = tuple((jnp.stack([shares[0][member]]) for member in range(6)))
    return (
        block_output,
        grad_stream,
        stacked[0],
        stacked[1],
        stacked[2],
        stacked[3],
        stacked[4],
        stacked[5],
    )


def solution(mesh):
    in_specs = (
        P(("rep", "fsdp"), None),
        P(("rep", "fsdp")),
        P(None, None, "fsdp"),
        P(None, None, "fsdp"),
        P(None, "fsdp", None),
        P(None, "fsdp", None),
        P(None, "fsdp", None),
        P(None, "fsdp", None),
        P(("rep", "fsdp"), None),
    )
    out_specs = (
        P(("rep", "fsdp"), None),
        P(("rep", "fsdp"), None),
        P(None, None, "fsdp"),
        P(None, None, "fsdp"),
        P(None, "fsdp", None),
        P(None, "fsdp", None),
        P(None, "fsdp", None),
        P(None, "fsdp", None),
    )
    return jax.shard_map(body, mesh=mesh, in_specs=in_specs, out_specs=out_specs, check_vma=False)
```

profile of v0, /device:TPU:1, one launch (start us, length us, event | category | flops | bytes accessed | tf_op | source)
XLA Modules:
  0.0 1419.2 jit_solution(9998316927995709905)
XLA Ops:
  7.2 2.1 copy.53
  11.1 2.3 copy.56
  14.3 83.0 %all-gather.1 = bf16[1,2,1088]{1,0,2:T(2,128)(2,1)S(1)} all-gather(bf16[1,2,34]{1,0,2:T(2,128)(2,1)S(1)} %copy.52), channel_id=3, replica_groups=mesh['rep'=4,'fsdp'=32] {'fsdp'}, dimensions={2}, use_global_device_ids=true | all-gather | bytes 4488 | tf_op jit(solution)/shard_map/all_gather | solution.py:162
  98.0 74.4 %all-gather = bf16[1,2,1088]{1,0,2:T(2,128)(2,1)S(1)} all-gather(bf16[1,2,34]{1,0,2:T(2,128)(2,1)S(1)} %copy.51), channel_id=2, replica_groups=mesh['rep'=4,'fsdp'=32] {'fsdp'}, dimensions={2}, use_global_device_ids=true | all-gather | bytes 4488 | tf_op jit(solution)/shard_map/all_gather | solution.py:161
  173.4 17.8 %slice_reduce_fusion = (f32[1088]{0:T(1024)S(1)}, f32[1088]{0:T(1024)S(1)}) fusion(f32[1,2,1088]{1,0,2:T(1,128)S(1)} %convert_element_type.146), kind=kLoop, calls=%fused_computation.79 | loop fusion | bytes 17408 | tf_op jit(solution)/shard_map/slice | solution.py:68
  191.3 18.0 %slice_reduce_fusion.1 = (f32[1088]{0:T(1024)S(1)}, f32[1088]{0:T(1024)S(1)}) fusion(f32[1,2,1088]{1,0,2:T(1,128)S(1)} %convert_element_type.145), kind=kLoop, calls=%fused_computation.80 | loop fusion | bytes 17408 | tf_op jit(solution)/shard_map/slice | solution.py:68
  209.3 8.4 fusion.15
  218.7 119.9 %all-gather.17.cloned.1.call-done = bf16[1,1088,1088]{2,0,1:T(2,128)(2,1)} async-done(((bf16[1,34,1088]{2,0,1:T(2,128)(2,1)}), bf16[1,1088,1088]{2,0,1:T(2,128)(2,1)}) %all-gather.17.cloned.1.call-update) | async-done | bytes 2367504 | tf_op jit(solution)/shard_map/all_gather | solution.py:164
  338.6 3.5 fusion.82
  342.3 231.8 %all-gather.19.cloned.1.call-done = bf16[1,1088,4352]{2,0,1:T(2,128)(2,1)} async-done(((bf16[1,34,4352]{2,0,1:T(2,128)(2,1)}), bf16[1,1088,4352]{2,0,1:T(2,128)(2,1)}) %all-gather.19.cloned.1.call-update) | async-done | bytes 9469968 | tf_op jit(solution)/shard_map/all_gather | solution.py:165
  574.1 15.5 %multiply_convert_fusion = (bf16[128,4352]{1,0:T(8,128)(2,1)S(1)}, f32[128,4352]{1,0:T(8,128)}) fusion(bf16[1,1088,4352]{2,0,1:T(2,128)(2,1)} %all-gather.19.cloned.1.call-done, f32[128,1088]{0,1:T(8,128)S(1)} %get-tuple-element.60, f32[1088]{0:T(1024)S(1)} %get-tuple-element.41, f32[1088]{0:T(1024)S(1)} %get-tuple-element.39, f32[128]{0:T(128)S(1)} %fusion.74, ...), kind=kOutput, calls=%fused_computation.31 | convolution fusion | flops 1249058816 | bytes 13379072 | tf_op jit(solution)/shard_map/dot_general | solution.py:69
  589.6 5.3 convolution_convert_fusion
  598.1 124.8 %all-gather.21.cloned.1.call-done = bf16[1,4352,1088]{2,1,0:T(8,128)(2,1)} async-done(((bf16[1,136,1088]{2,1,0:T(8,128)(2,1)}), bf16[1,4352,1088]{2,1,0:T(8,128)(2,1)}) %all-gather.21.cloned.1.call-update) | async-done | bytes 9469968 | tf_op jit(solution)/shard_map/all_gather | solution.py:166
  722.9 9.4 add_convert_fusion
  732.3 9.1 multiply_reduce_fusion
  745.9 5.1 convolution_convert_fusion.2
  751.0 5.7 convolution_convert_fusion.1
  756.7 347.1 %fusion.78 = (bf16[40,3264]{1,0:T(8,128)(2,1)}, bf16[48,1088]{1,0:T(8,128)(2,1)S(1)}, bf16[40,4352]{1,0:T(8,128)(2,1)}) fusion(bf16[1088,3264]{1,0:T(8,128)(2,1)} %convolution_convert_fusion.2, bf16[1088,1088]{1,0:T(8,128)(2,1)S(1)} %convolution_convert_fusion.3, bf16[1088,4352]{1,0:T(8,128)(2,1)} %convolution_convert_fusion.1), kind=kCustom, calls=%all-reduce-scatter.3 | all-reduce-scatter fusion | flops 11419650 | bytes 19654144
  1106.4 6.0 collective-permute-start.11
  1112.5 3.8 collective-permute-start.10
  1116.4 7.5 fusion.77
  1124.3 2.1 collective-permute-start.14
  1127.2 3.7 collective-permute-start.9
  1130.9 2.6 collective-permute-start.8
  1133.5 9.0 collective-permute-start.7
  1143.8 66.8 %all-reduce.10 = (bf16[2,1088]{1,0:T(2,128)(2,1)S(1)}, bf16[2,1088]{1,0:T(2,128)(2,1)S(1)}) all-reduce(bf16[2,1088]{1,0:T(2,128)(2,1)S(1)} %pad_maximum_fusion.1, bf16[2,1088]{1,0:T(2,128)(2,1)S(1)} %pad_maximum_fusion.2), channel_id=8, replica_groups=mesh['rep'=4,'fsdp'=32] {'fsdp'}, use_global_device_ids=true, to_apply=%region_13.14.clone | all-reduce | flops 4352 | bytes 17408
  1210.7 2.0 collective-permute-start.5
  1212.7 2.0 collective-permute-start.3
  1216.7 2.0 collective-permute-start.1
  1218.7 2.6 collective-permute-start
  1222.9 34.0 %all-reduce.9 = (f32[1,2,34]{2,1,0:T(2,128)}, f32[1,2,34]{2,1,0:T(2,128)}) all-reduce(f32[1,2,34]{2,1,0:T(2,128)S(1)} %get-tuple-element.65, f32[1,2,34]{2,1,0:T(2,128)S(1)} %get-tuple-element.66), channel_id=1, replica_groups=mesh['rep'=4,'fsdp'=32] {'rep'}, use_global_device_ids=true, to_apply=%region_14.15 | all-reduce | flops 136 | bytes 1088 | tf_op jit(solution)/shard_map/psum | solution.py:225
  1259.6 8.8 concatenate.1
  1269.4 2.0 collective-permute-start.18
  1271.4 2.1 collective-permute-start.17
  1273.6 2.3 collective-permute-start.16
  1275.9 2.8 collective-permute-start.15
  1278.7 9.8 collective-permute-start.19
  1288.5 11.0 concatenate
  1300.3 2.2 copy.77
  1302.6 23.2 %concatenate.2 = bf16[226,4352]{1,0:T(8,128)(2,1)} concatenate(bf16[26,4352]{1,0:T(8,128)(2,1)} %collective-permute-done.19, bf16[40,4352]{1,0:T(8,128)(2,1)} %collective-permute-done.18, bf16[40,4352]{1,0:T(8,128)(2,1)} %collective-permute-done.17, bf16[40,4352]{1,0:T(8,128)(2,1)} %collective-permute-done.16, bf16[40,4352]{1,0:T(8,128)(2,1)} %collective-permute-done.15, ...), dimensions={0} | concatenate | bytes 3934208
  1328.8 7.5 fusion.28
  1336.4 2.0 copy.83
  1340.5 9.4 all-gather.7
  1352.0 7.8 all-gather.6
  1361.4 8.7 reduce-scatter.29.cloned.1.call-done
  1371.2 8.3 all-gather.8
  1381.5 20.0 %reduce-scatter.31.cloned.1.call-done = bf16[272,136]{1,0:T(8,128)(2,1)} async-done(((bf16[1088,136]{1,0:T(8,128)(2,1)}), bf16[272,136]{1,0:T(8,128)(2,1)}) %reduce-scatter.31.cloned.1.call-update) | async-done | bytes 74000
  1402.5 8.4 all-gather.9
  (168 shorter events, 38.5 us)
Async XLA Ops:
  7.2 6.9 copy-start.24
  7.2 7.0 copy-start.25
  7.2 202.2 %all-gather.15.cloned.1.call-start = ((), (), s32[]{:S(2)}) async-start(), calls=%async_computation.5 | async-start | bytes 14936064 | tf_op jit(solution)/shard_map/all_gather | solution.py:163
  9.3 329.3 %all-gather.17.cloned.1.call-start = ((), (), s32[]{:S(2)}) async-start(), calls=%async_computation.6 | async-start | bytes 5170176 | tf_op jit(solution)/shard_map/all_gather | solution.py:164
  11.1 563.0 %all-gather.19.cloned.1.call-start = ((), (), s32[]{:S(2)}) async-start(), calls=%async_computation.7 | async-start | bytes 19531776 | tf_op jit(solution)/shard_map/all_gather | solution.py:165
  13.4 159.6 %copy-start = (bf16[128,1088]{0,1:T(8,128)(2,1)S(1)}, bf16[128,1088]{0,1:T(8,128)(2,1)}, u32[]{:S(2)}) copy-start(bf16[128,1088]{0,1:T(8,128)(2,1)} %param.9) | copy-start | bytes 835588
  13.4 159.9 %copy-start.22 = (s32[128]{0:T(128)S(1)}, s32[128]{0:T(128)}, u32[]{:S(2)}) copy-start(s32[128]{0:T(128)} %param.10) | copy-start | bytes 1540
  13.4 709.5 %all-gather.21.cloned.1.call-start = ((), (), s32[]{:S(2)}) async-start(), calls=%async_computation.8 | async-start | bytes 10340352 | tf_op jit(solution)/shard_map/all_gather | solution.py:166
  14.0 1322.4 %reduce-scatter.33.cloned.1.call-start = ((), (), s32[]{:S(2)}) async-start(), calls=%async_computation.13 | async-start | bytes 10340352
  218.7 123.6 %copy-start.9 = (bf16[17,64,128]{2,1,0:T(8,128)(2,1)}, bf16[17,64,128]{2,1,0:T(8,128)(2,1)S(1)}, u32[]{:S(2)}) copy-start(bf16[17,64,128]{2,1,0:T(8,128)(2,1)S(1)} %convolution_convert_fusion.7) | copy-start | bytes 835588
  574.1 15.5 %copy-start.7 = (bf16[128,1088]{0,1:T(8,128)(2,1)S(1)}, bf16[128,1088]{0,1:T(8,128)(2,1)}, u32[]{:S(2)}) copy-start(bf16[128,1088]{0,1:T(8,128)(2,1)} %param.17) | copy-start | bytes 835588
  595.0 744.5 %reduce-scatter.27.cloned.1.call-start = ((), (), s32[]{:S(2)}) async-start(), calls=%async_computation.10 | async-start | bytes 348160
  722.9 18.9 %slice-start = ((s8[5013504]{0:T(1024)(128)(4,1)}), s8[4194304]{0:T(1024)(128)(4,1)S(1)}, s32[]{:S(2)}) async-start(s8[5013504]{0:T(1024)(128)(4,1)} %bitcast.195), calls=%async_computation.14 | async-start | bytes 8388608
  722.9 18.9 %slice-start.1 = ((s8[5013504]{0:T(1024)(128)(4,1)}), s8[819200]{0:T(1024)(128)(4,1)S(1)}, s32[]{:S(2)}) async-start(s8[5013504]{0:T(1024)(128)(4,1)} %bitcast.195), calls=%async_computation.15 | async-start | bytes 1638400
  1103.8 27.1 %collective-permute-start.13 = (bf16[48,1088]{1,0:T(8,128)(2,1)S(1)}, bf16[48,1088]{1,0:T(8,128)(2,1)S(1)}, u32[]{:S(2)}, u32[]{:S(2)}) collective-permute-start(bf16[48,1088]{1,0:T(8,128)(2,1)S(1)} %get-tuple-element.51), channel_id=1, source_target_pairs={{0,9},{1,10},{2,11},{3,12},{4,13},{5,14},{6,15},{7,16},{8,17},{9,1... | collective-permute-start | bytes 313352
  1105.1 28.4 %collective-permute-start.12 = (bf16[48,1088]{1,0:T(8,128)(2,1)S(1)}, bf16[48,1088]{1,0:T(8,128)(2,1)S(1)}, u32[]{:S(2)}, u32[]{:S(2)}) collective-permute-start(bf16[48,1088]{1,0:T(8,128)(2,1)S(1)} %get-tuple-element.51), channel_id=1, source_target_pairs={{0,8},{1,9},{2,10},{3,11},{4,12},{5,13},{6,14},{7,15},{8,16},{9,17... | collective-permute-start | bytes 313352
  1106.4 36.1 %collective-permute-start.11 = (bf16[48,1088]{1,0:T(8,128)(2,1)S(1)}, bf16[48,1088]{1,0:T(8,128)(2,1)S(1)}, u32[]{:S(2)}, u32[]{:S(2)}) collective-permute-start(bf16[48,1088]{1,0:T(8,128)(2,1)S(1)} %get-tuple-element.51), channel_id=1, source_target_pairs={{0,7},{1,8},{2,9},{3,10},{4,11},{5,12},{6,13},{7,14},{8,15},{9,16}... | collective-permute-start | bytes 313352
  1112.5 98.2 %collective-permute-start.10 = (bf16[48,1088]{1,0:T(8,128)(2,1)S(1)}, bf16[48,1088]{1,0:T(8,128)(2,1)S(1)}, u32[]{:S(2)}, u32[]{:S(2)}) collective-permute-start(bf16[48,1088]{1,0:T(8,128)(2,1)S(1)} %get-tuple-element.51), channel_id=1, source_target_pairs={{0,6},{1,7},{2,8},{3,9},{4,10},{5,11},{6,12},{7,13},{8,14},{9,15},... | collective-permute-start | bytes 313352
  1116.4 96.3 %copy-start.11 = (bf16[40,3264]{1,0:T(8,128)(2,1)S(1)}, bf16[40,3264]{1,0:T(8,128)(2,1)}, u32[]{:S(2)}) copy-start(bf16[40,3264]{1,0:T(8,128)(2,1)} %get-tuple-element.50) | copy-start | bytes 783364
  1116.4 105.8 %copy-start.6 = (bf16[40,4352]{1,0:T(8,128)(2,1)S(1)}, bf16[40,4352]{1,0:T(8,128)(2,1)}, u32[]{:S(2)}) copy-start(bf16[40,4352]{1,0:T(8,128)(2,1)} %get-tuple-element.52) | copy-start | bytes 1044484
  1124.3 2.9 collective-permute-start.14
  1127.2 85.5 %collective-permute-start.9 = (bf16[48,1088]{1,0:T(8,128)(2,1)S(1)}, bf16[48,1088]{1,0:T(8,128)(2,1)S(1)}, u32[]{:S(2)}, u32[]{:S(2)}) collective-permute-start(bf16[48,1088]{1,0:T(8,128)(2,1)S(1)} %get-tuple-element.51), channel_id=1, source_target_pairs={{0,5},{1,6},{2,7},{3,8},{4,9},{5,10},{6,11},{7,12},{8,13},{9,14},{... | collective-permute-start | bytes 313352
  1130.9 83.8 %collective-permute-start.8 = (bf16[48,1088]{1,0:T(8,128)(2,1)S(1)}, bf16[48,1088]{1,0:T(8,128)(2,1)S(1)}, u32[]{:S(2)}, u32[]{:S(2)}) collective-permute-start(bf16[48,1088]{1,0:T(8,128)(2,1)S(1)} %get-tuple-element.51), channel_id=1, source_target_pairs={{0,4},{1,5},{2,6},{3,7},{4,8},{5,9},{6,10},{7,11},{8,12},{9,13},{1... | collective-permute-start | bytes 313352
  1133.5 123.4 %copy-start.14 = (bf16[48,1088]{1,0:T(8,128)(2,1)}, bf16[48,1088]{1,0:T(8,128)(2,1)S(1)}, u32[]{:S(2)}) copy-start(bf16[48,1088]{1,0:T(8,128)(2,1)S(1)} %collective-permute-done.12) | copy-start | bytes 313348
  1133.5 83.2 %collective-permute-start.7 = (bf16[48,1088]{1,0:T(8,128)(2,1)S(1)}, bf16[48,1088]{1,0:T(8,128)(2,1)S(1)}, u32[]{:S(2)}, u32[]{:S(2)}) collective-permute-start(bf16[48,1088]{1,0:T(8,128)(2,1)S(1)} %get-tuple-element.51), channel_id=1, source_target_pairs={{0,3},{1,4},{2,5},{3,6},{4,7},{5,8},{6,9},{7,10},{8,11},{9,12},{10... | collective-permute-start | bytes 313352
  1142.5 114.4 %copy-start.15 = (bf16[48,1088]{1,0:T(8,128)(2,1)}, bf16[48,1088]{1,0:T(8,128)(2,1)S(1)}, u32[]{:S(2)}) copy-start(bf16[48,1088]{1,0:T(8,128)(2,1)S(1)} %collective-permute-done.11) | copy-start | bytes 313348
  1142.5 76.2 %collective-permute-start.6 = (bf16[48,1088]{1,0:T(8,128)(2,1)S(1)}, bf16[48,1088]{1,0:T(8,128)(2,1)S(1)}, u32[]{:S(2)}, u32[]{:S(2)}) collective-permute-start(bf16[48,1088]{1,0:T(8,128)(2,1)S(1)} %get-tuple-element.51), channel_id=1, source_target_pairs={{0,2},{1,3},{2,4},{3,5},{4,6},{5,7},{6,8},{7,9},{8,10},{9,11},{10,... | collective-permute-start | bytes 313352
  1210.6 46.2 %copy-start.16 = (bf16[48,1088]{1,0:T(8,128)(2,1)}, bf16[48,1088]{1,0:T(8,128)(2,1)S(1)}, u32[]{:S(2)}) copy-start(bf16[48,1088]{1,0:T(8,128)(2,1)S(1)} %collective-permute-done.10) | copy-start | bytes 313348
  1210.7 46.2 %collective-permute-start.5 = (bf16[48,1088]{1,0:T(8,128)(2,1)S(1)}, bf16[48,1088]{1,0:T(8,128)(2,1)S(1)}, u32[]{:S(2)}, u32[]{:S(2)}) collective-permute-start(bf16[48,1088]{1,0:T(8,128)(2,1)S(1)} %get-tuple-element.51), channel_id=1, source_target_pairs={{0,1},{1,2},{2,3},{3,4},{4,5},{5,6},{6,7},{7,8},{8,9},{9,10},{10,1... | collective-permute-start | bytes 313352
  1212.7 44.2 %copy-start.17 = (bf16[48,1088]{1,0:T(8,128)(2,1)}, bf16[48,1088]{1,0:T(8,128)(2,1)S(1)}, u32[]{:S(2)}) copy-start(bf16[48,1088]{1,0:T(8,128)(2,1)S(1)} %collective-permute-done.9) | copy-start | bytes 313348
  1212.7 58.8 %collective-permute-start.3 = (bf16[40,3264]{1,0:T(8,128)(2,1)S(1)}, bf16[40,3264]{1,0:T(8,128)(2,1)}, u32[]{:S(2)}, u32[]{:S(2)}) collective-permute-start(bf16[40,3264]{1,0:T(8,128)(2,1)S(1)} %copy-done.11), channel_id=1, source_target_pairs={{0,4},{1,5},{2,6},{3,7},{4,8},{5,9},{6,10},{7,11},{8,12},{9,13},{1... | collective-permute-start | bytes 783368
  1214.7 42.2 %copy-start.18 = (bf16[48,1088]{1,0:T(8,128)(2,1)}, bf16[48,1088]{1,0:T(8,128)(2,1)S(1)}, u32[]{:S(2)}) copy-start(bf16[48,1088]{1,0:T(8,128)(2,1)S(1)} %collective-permute-done.8) | copy-start | bytes 313348
  1214.7 58.9 %collective-permute-start.2 = (bf16[40,3264]{1,0:T(8,128)(2,1)S(1)}, bf16[40,3264]{1,0:T(8,128)(2,1)}, u32[]{:S(2)}, u32[]{:S(2)}) collective-permute-start(bf16[40,3264]{1,0:T(8,128)(2,1)S(1)} %copy-done.11), channel_id=1, source_target_pairs={{0,3},{1,4},{2,5},{3,6},{4,7},{5,8},{6,9},{7,10},{8,11},{9,12},{10... | collective-permute-start | bytes 783368
  1216.7 40.2 %copy-start.19 = (bf16[48,1088]{1,0:T(8,128)(2,1)}, bf16[48,1088]{1,0:T(8,128)(2,1)S(1)}, u32[]{:S(2)}) copy-start(bf16[48,1088]{1,0:T(8,128)(2,1)S(1)} %collective-permute-done.7) | copy-start | bytes 313348
  1216.7 59.2 %collective-permute-start.1 = (bf16[40,3264]{1,0:T(8,128)(2,1)S(1)}, bf16[40,3264]{1,0:T(8,128)(2,1)}, u32[]{:S(2)}, u32[]{:S(2)}) collective-permute-start(bf16[40,3264]{1,0:T(8,128)(2,1)S(1)} %copy-done.11), channel_id=1, source_target_pairs={{0,2},{1,3},{2,4},{3,5},{4,6},{5,7},{6,8},{7,9},{8,10},{9,11},{10,... | collective-permute-start | bytes 783368
  1218.7 38.2 %copy-start.20 = (bf16[48,1088]{1,0:T(8,128)(2,1)}, bf16[48,1088]{1,0:T(8,128)(2,1)S(1)}, u32[]{:S(2)}) copy-start(bf16[48,1088]{1,0:T(8,128)(2,1)S(1)} %collective-permute-done.6) | copy-start | bytes 313348
  1218.7 60.0 %collective-permute-start = (bf16[40,3264]{1,0:T(8,128)(2,1)S(1)}, bf16[40,3264]{1,0:T(8,128)(2,1)}, u32[]{:S(2)}, u32[]{:S(2)}) collective-permute-start(bf16[40,3264]{1,0:T(8,128)(2,1)S(1)} %copy-done.11), channel_id=1, source_target_pairs={{0,1},{1,2},{2,3},{3,4},{4,5},{5,6},{6,7},{7,8},{8,9},{9,10},{10,1... | collective-permute-start | bytes 783368
  1257.6 11.8 collective-permute-start.4
  1269.3 81.6 %reduce-scatter.25.cloned.1.call-start = ((), (), s32[]{:S(2)}) async-start(), calls=%async_computation.9 | async-start | bytes 1044480
  1269.4 33.2 %collective-permute-start.18 = (bf16[40,4352]{1,0:T(8,128)(2,1)S(1)}, bf16[40,4352]{1,0:T(8,128)(2,1)}, u32[]{:S(2)}, u32[]{:S(2)}) collective-permute-start(bf16[40,4352]{1,0:T(8,128)(2,1)S(1)} %copy-done.6), channel_id=1, source_target_pairs={{0,4},{1,5},{2,6},{3,7},{4,8},{5,9},{6,10},{7,11},{8,12},{9,13},{1... | collective-permute-start | bytes 1044488
  1271.4 31.2 %collective-permute-start.17 = (bf16[40,4352]{1,0:T(8,128)(2,1)S(1)}, bf16[40,4352]{1,0:T(8,128)(2,1)}, u32[]{:S(2)}, u32[]{:S(2)}) collective-permute-start(bf16[40,4352]{1,0:T(8,128)(2,1)S(1)} %copy-done.6), channel_id=1, source_target_pairs={{0,3},{1,4},{2,5},{3,6},{4,7},{5,8},{6,9},{7,10},{8,11},{9,12},{10... | collective-permute-start | bytes 1044488
  1273.6 29.0 %collective-permute-start.16 = (bf16[40,4352]{1,0:T(8,128)(2,1)S(1)}, bf16[40,4352]{1,0:T(8,128)(2,1)}, u32[]{:S(2)}, u32[]{:S(2)}) collective-permute-start(bf16[40,4352]{1,0:T(8,128)(2,1)S(1)} %copy-done.6), channel_id=1, source_target_pairs={{0,2},{1,3},{2,4},{3,5},{4,6},{5,7},{6,8},{7,9},{8,10},{9,11},{10,... | collective-permute-start | bytes 1044488
  1275.9 26.7 %collective-permute-start.15 = (bf16[40,4352]{1,0:T(8,128)(2,1)S(1)}, bf16[40,4352]{1,0:T(8,128)(2,1)}, u32[]{:S(2)}, u32[]{:S(2)}) collective-permute-start(bf16[40,4352]{1,0:T(8,128)(2,1)S(1)} %copy-done.6), channel_id=1, source_target_pairs={{0,1},{1,2},{2,3},{3,4},{4,5},{5,6},{6,7},{7,8},{8,9},{9,10},{10,1... | collective-permute-start | bytes 1044488
  1278.7 23.8 %collective-permute-start.19 = (bf16[26,4352]{1,0:T(8,128)(2,1)}, bf16[26,4352]{1,0:T(8,128)(2,1)}, u32[]{:S(2)}, u32[]{:S(2)}) collective-permute-start(bf16[26,4352]{1,0:T(8,128)(2,1)} %slice.46), channel_id=1, source_target_pairs={{0,5},{1,6},{2,7},{3,8},{4,9},{5,10},{6,11},{7,12},{8,13},{9,14},{... | collective-permute-start | bytes 678920
  1302.5 67.6 %reduce-scatter.29.cloned.1.call-start = ((), (), s32[]{:S(2)}) async-start(), calls=%async_computation.11 | async-start | bytes 1392640
  1328.5 9.9 copy-start.4
  1328.5 9.9 copy-start.8
  1328.5 73.0 %reduce-scatter.31.cloned.1.call-start = ((), (), s32[]{:S(2)}) async-start(), calls=%async_computation.12 | async-start | bytes 696320
  (9 other events, 14.8 us)
Sparse Core Ops, SparseCore 0:
  10.2 174.8 all-gather.14
  187.3 151.2 all-gather.16
  340.8 233.2 all-gather.18
  575.6 147.2 all-gather.20
  725.2 233.5 reduce-scatter.32
  1269.5 31.2 reduce-scatter.26
  1303.4 32.4 reduce-scatter.24
  1338.5 31.5 reduce-scatter.28
  1373.3 28.1 reduce-scatter.30
where the time goes:
time: 1430 us; the launch traced here: 1420 us
  blocking collectives  639 us (45%)
  waiting for transfers between devices  507 us (35%)
  local copies, waits for them, and re-layouts  108 us (8%)
  matrix products  81.1 us (6%)
  starting transfers between devices  63.5 us (4%)
  between operations  17 us (1%)
    unnamed x2, blocking collectives  414 us
    all_gather x1, waiting for transfers between devices, body(): lax.all_gather(w_fc1[layer_idx], 'fsdp', axis=0, tiled=True)  232 us
    all_gather x1, waiting for transfers between devices, body(): lax.all_gather(w_fc2[layer_idx], 'fsdp', axis=0, tiled=True)  125 us
    all_gather x1, waiting for transfers between devices, body(): lax.all_gather(w_out[layer_idx], 'fsdp', axis=0, tiled=True)  120 us
    all_gather x1, blocking collectives, body(): lax.all_gather(ln_bias[layer_idx], 'fsdp', axis=1, tiled=True)  83 us
    all_gather x1, blocking collectives, body(): lax.all_gather(ln_gain[layer_idx], 'fsdp', axis=1, tiled=True)  74.4 us
    unnamed x82, local copies, waits for them, and re-layouts  69.4 us
    unnamed x25, starting transfers between devices  63.3 us
  transfers between devices with their start and end apart: 29, of which 6 were waited for; matrix products, arithmetic and copies ran while one was open for 38% of the time, Pallas kernels for 0%

commit v1 on v0

--- a/solution.py
+++ b/solution.py
@@ -153,6 +153,12 @@
 
 
 def body(tokens, segments, ln_gain, ln_bias, w_qkv, w_out, w_fc1, w_fc2, cotangent):
+
+    def group_the_trees(local):
+        return jnp.concatenate(
+            lax.all_to_all(jnp.stack(lax.axis_size("fsdp") * [local]), "fsdp", 0, 0), 0
+        )
+
     row_count = tokens.shape[0]
     allowed = allowed_mask(segments.reshape(row_count // SEQ, SEQ))
     stream = tokens.astype(jnp.float32)
@@ -162,7 +168,7 @@
         lax.all_gather(ln_bias[layer_idx], "fsdp", axis=1, tiled=True),
         lax.all_gather(w_qkv[layer_idx], "fsdp", axis=0, tiled=True),
         lax.all_gather(w_out[layer_idx], "fsdp", axis=0, tiled=True),
-        lax.all_gather(w_fc1[layer_idx], "fsdp", axis=0, tiled=True),
+        group_the_trees(w_fc1[layer_idx]),
         lax.all_gather(w_fc2[layer_idx], "fsdp", axis=0, tiled=True),
     )
     stream, kept_acts = forward_layer(stream, allowed, whole_set)

time: 1430 us -> 1360 us (0.951)
  waiting for transfers between devices: 507 us -> 203 us
  blocking collectives: 639 us -> 840 us
  local copies, waits for them, and re-layouts: 108 us -> 135 us
    all_gather x1 -> x0, waiting for transfers between devices: 232 us -> none  [body(): lax.all_gather(w_fc1[layer_idx], 'fsdp', axis=0, tiled=True)]
    all_gather x1, blocking collectives: 83 us -> 291 us  [body(): lax.all_gather(ln_bias[layer_idx], 'fsdp', axis=1, tiled=True)]
    all_gather x1, waiting for transfers between devices: 120 us -> 28.8 us  [body(): lax.all_gather(w_out[layer_idx], 'fsdp', axis=0, tiled=True)]
    all_gather x1, waiting for transfers between devices: 125 us -> 147 us  [body(): lax.all_gather(w_fc2[layer_idx], 'fsdp', axis=0, tiled=True)]
    unnamed x82 -> x81, local copies, waits for them, and re-layouts: 69.4 us -> 79.5 us
    unnamed x34 -> x33, waiting for transfers between devices: 30.1 us -> 27 us
  transfers between devices with their start and end apart: 29 -> 29, of which waited for: 6 -> 5; matrix products, arithmetic and copies ran while one was open for 38% -> 41% of each run, Pallas kernels for 0% -> 0%
where the time goes in v1:
time: 1360 us; the launch traced here: 1350 us
  blocking collectives  840 us (62%)
  waiting for transfers between devices  203 us (15%)
  local copies, waits for them, and re-layouts  135 us (10%)
  matrix products  78.8 us (6%)
  starting transfers between devices  71.7 us (5%)
  between operations  17.3 us (1%)
    unnamed x2, blocking collectives  412 us
    all_gather x1, blocking collectives, body(): lax.all_gather(ln_bias[layer_idx], 'fsdp', axis=1, tiled=True)  291 us
    all_gather x1, waiting for transfers between devices, body(): lax.all_gather(w_fc2[layer_idx], 'fsdp', axis=0, tiled=True)  147 us
    unnamed x81, local copies, waits for them, and re-layouts  79.5 us
    all_gather x1, blocking collectives, body(): lax.all_gather(ln_gain[layer_idx], 'fsdp', axis=1, tiled=True)  69 us
    unnamed x25, starting transfers between devices  61.6 us
    psum x1, blocking collectives, body(): norm_terms = lax.psum((summed_part[0], summed_part[1]), 'rep')  33.3 us
    all_gather x1, waiting for transfers between devices, body(): lax.all_gather(w_out[layer_idx], 'fsdp', axis=0, tiled=True)  28.8 us
  transfers between devices with their start and end apart: 29, of which 5 were waited for; matrix products, arithmetic and copies ran while one was open for 41% of the time, Pallas kernels for 0%

profile of v1, /device:TPU:1, one launch (start us, length us, event | category | flops | bytes accessed | tf_op | source)
XLA Modules:
  0.0 1351.0 jit_solution(3637587420638173629)
XLA Ops:
  7.2 2.1 copy.52
  11.8 5.8 stack.65
  17.6 10.0 all-to-all-start
  27.8 291.2 %all-gather.1 = bf16[1,2,1088]{1,0,2:T(2,128)(2,1)S(1)} all-gather(bf16[1,2,34]{1,0,2:T(2,128)(2,1)S(1)} %copy.51), channel_id=3, replica_groups=mesh['rep'=4,'fsdp'=32] {'fsdp'}, dimensions={2}, use_global_device_ids=true | all-gather | bytes 4488 | tf_op jit(solution)/shard_map/all_gather | solution.py:168
  319.7 69.0 %all-gather = bf16[1,2,1088]{1,0,2:T(2,128)(2,1)S(1)} all-gather(bf16[1,2,34]{1,0,2:T(2,128)(2,1)S(1)} %copy.50), channel_id=2, replica_groups=mesh['rep'=4,'fsdp'=32] {'fsdp'}, dimensions={2}, use_global_device_ids=true | all-gather | bytes 4488 | tf_op jit(solution)/shard_map/all_gather | solution.py:167
  389.8 17.8 %slice_reduce_fusion = (f32[1088]{0:T(1024)S(1)}, f32[1088]{0:T(1024)S(1)}) fusion(f32[1,2,1088]{1,0,2:T(1,128)S(1)} %convert_element_type.146), kind=kLoop, calls=%fused_computation.73 | loop fusion | bytes 17408 | tf_op jit(solution)/shard_map/slice | solution.py:68
  407.6 18.1 %slice_reduce_fusion.1 = (f32[1088]{0:T(1024)S(1)}, f32[1088]{0:T(1024)S(1)}) fusion(f32[1,2,1088]{1,0,2:T(1,128)S(1)} %convert_element_type.145), kind=kLoop, calls=%fused_computation.74 | loop fusion | bytes 17408 | tf_op jit(solution)/shard_map/slice | solution.py:68
  425.7 10.9 reshape.250
  436.6 8.4 fusion.11
  446.3 28.8 %all-gather.15.cloned.1.call-done = bf16[1,1088,1088]{2,0,1:T(2,128)(2,1)} async-done(((bf16[1,34,1088]{2,0,1:T(2,128)(2,1)}), bf16[1,1088,1088]{2,0,1:T(2,128)(2,1)}) %all-gather.15.cloned.1.call-update) | async-done | bytes 2367504 | tf_op jit(solution)/shard_map/all_gather | solution.py:170
  475.1 3.5 fusion.77
  478.8 9.9 multiply_convert_fusion
  489.7 5.3 convolution_convert_fusion
  498.2 147.5 %all-gather.17.cloned.1.call-done = bf16[1,4352,1088]{2,1,0:T(8,128)(2,1)} async-done(((bf16[1,136,1088]{2,1,0:T(8,128)(2,1)}), bf16[1,4352,1088]{2,1,0:T(8,128)(2,1)}) %all-gather.17.cloned.1.call-update) | async-done | bytes 9469968 | tf_op jit(solution)/shard_map/all_gather | solution.py:172
  645.7 17.8 %add_convert_fusion = bf16[128,4352]{1,0:T(8,128)(2,1)S(1)} fusion(bf16[128,1088]{0,1:T(8,128)(2,1)S(1)} %copy-done.5, bf16[1,4352,1088]{2,1,0:T(8,128)(2,1)} %all-gather.17.cloned.1.call-done, f32[128,4352]{1,0:T(8,128)} %get-tuple-element.62), kind=kOutput, calls=%fused_computation.24 | convolution fusion | flops 1252261888 | bytes 13090816 | tf_op jit(solution)/shard_map/dot_general | solution.py:28
  663.5 2.8 multiply_reduce_fusion
  669.9 2.3 convolution_convert_fusion.3
  672.2 5.1 convolution_convert_fusion.2
  677.4 5.4 convolution_convert_fusion.1
  682.8 346.1 %fusion.73 = (bf16[40,3264]{1,0:T(8,128)(2,1)S(1)}, bf16[48,1088]{1,0:T(8,128)(2,1)S(1)}, bf16[40,4352]{1,0:T(8,128)(2,1)S(1)}) fusion(bf16[1088,3264]{1,0:T(8,128)(2,1)} %convolution_convert_fusion.2, bf16[1088,1088]{1,0:T(8,128)(2,1)} %convolution_convert_fusion.3, bf16[1088,4352]{1,0:T(8,128)(2,1)} %convolution_convert_fusion.1), kind=kCustom, calls=%all-reduce-scatter.3 | all-reduce-scatter fusion | flops 11419650 | bytes 19654144
  1031.5 6.6 collective-permute-start.11
  1038.2 1.9 collective-permute-start.10
  1040.1 7.3 fusion.72
  1049.9 4.1 collective-permute-start.9
  1054.0 1.9 collective-permute-start.8
  1056.0 9.0 collective-permute-start.7
  1066.9 66.3 %all-reduce.10 = (bf16[2,1088]{1,0:T(2,128)(2,1)S(1)}, bf16[2,1088]{1,0:T(2,128)(2,1)S(1)}) all-reduce(bf16[2,1088]{1,0:T(2,128)(2,1)S(1)} %pad_maximum_fusion.1, bf16[2,1088]{1,0:T(2,128)(2,1)S(1)} %pad_maximum_fusion.2), channel_id=7, replica_groups=mesh['rep'=4,'fsdp'=32] {'fsdp'}, use_global_device_ids=true, to_apply=%region_13.14.clone | all-reduce | flops 4352 | bytes 17408
  1134.6 2.0 collective-permute-start.2
  1136.6 2.0 collective-permute-start.1
  1138.6 3.5 collective-permute-start
  1142.2 1.9 collective-permute-start.5
  1145.0 33.3 %all-reduce.9 = (f32[1,2,34]{2,1,0:T(2,128)}, f32[1,2,34]{2,1,0:T(2,128)}) all-reduce(f32[1,2,34]{2,1,0:T(2,128)S(1)} %get-tuple-element.65, f32[1,2,34]{2,1,0:T(2,128)S(1)} %get-tuple-element.66), channel_id=1, replica_groups=mesh['rep'=4,'fsdp'=32] {'rep'}, use_global_device_ids=true, to_apply=%region_14.15 | all-reduce | flops 136 | bytes 1088 | tf_op jit(solution)/shard_map/psum | solution.py:231
  1179.7 16.3 %concatenate.1 = bf16[482,1088]{1,0:T(8,128)(2,1)} concatenate(bf16[2,1088]{1,0:T(2,128)(2,1)S(1)} %collective-permute-done.14, bf16[48,1088]{1,0:T(8,128)(2,1)S(1)} %collective-permute-done.13, bf16[48,1088]{1,0:T(8,128)(2,1)S(1)} %collective-permute-done.12, bf16[48,1088]{1,0:T(8,128)(2,1)} %copy-done.11, bf16[48,1088]{1,0:T(8,128)(2,1)} %collective-permute-done.10, ...), dimensions={0} | concatenate | bytes 2097664
  1199.2 2.2 collective-permute-start.17
  1201.5 3.3 collective-permute-start.16
  1204.8 4.7 collective-permute-start.15
  1209.5 9.0 collective-permute-start.19
  1218.5 16.0 %concatenate = bf16[226,3264]{1,0:T(8,128)(2,1)} concatenate(bf16[26,3264]{1,0:T(8,128)(2,1)S(1)} %collective-permute-done.4, bf16[40,3264]{1,0:T(8,128)(2,1)S(1)} %collective-permute-done.3, bf16[40,3264]{1,0:T(8,128)(2,1)} %collective-permute-done.2, bf16[40,3264]{1,0:T(8,128)(2,1)} %collective-permute-done.1, bf16[40,3264]{1,0:T(8,128)(2,1)} %collective-permute-done, ...), dimensions={0} | concatenate | bytes 2950656
  1237.0 22.3 %concatenate.2 = bf16[226,4352]{1,0:T(8,128)(2,1)} concatenate(bf16[26,4352]{1,0:T(8,128)(2,1)} %collective-permute-done.19, bf16[40,4352]{1,0:T(8,128)(2,1)S(1)} %collective-permute-done.18, bf16[40,4352]{1,0:T(8,128)(2,1)S(1)} %collective-permute-done.17, bf16[40,4352]{1,0:T(8,128)(2,1)} %collective-permute-done.16, bf16[40,4352]{1,0:T(8,128)(2,1)} %collective-permute-done.15, ...), dimensions={0} | concatenate | bytes 3934208
  1262.0 7.6 fusion.22
  1269.7 2.0 copy.81
  1271.7 2.1 add_add_fusion.2
  1274.8 9.7 all-gather.6
  1286.6 7.8 all-gather.5
  1296.1 5.5 reduce-scatter.29.cloned.1.call-done
  1302.7 8.3 all-gather.7
  1312.9 20.0 %reduce-scatter.31.cloned.1.call-done = bf16[272,136]{1,0:T(8,128)(2,1)} async-done(((bf16[1088,136]{1,0:T(8,128)(2,1)}), bf16[272,136]{1,0:T(8,128)(2,1)}) %reduce-scatter.31.cloned.1.call-update) | async-done | bytes 74000
  1333.9 8.4 all-gather.8
  (169 shorter events, 40.6 us)
Async XLA Ops:
  7.2 429.5 %all-gather.13.cloned.1.call-start = ((), (), s32[]{:S(2)}) async-start(), calls=%async_computation.6 | async-start | bytes 14936064 | tf_op jit(solution)/shard_map/all_gather | solution.py:169
  9.3 465.8 %all-gather.15.cloned.1.call-start = ((), (), s32[]{:S(2)}) async-start(), calls=%async_computation.7 | async-start | bytes 5170176 | tf_op jit(solution)/shard_map/all_gather | solution.py:170
  11.1 634.6 %all-gather.17.cloned.1.call-start = ((), (), s32[]{:S(2)}) async-start(), calls=%async_computation.8 | async-start | bytes 10340352 | tf_op jit(solution)/shard_map/all_gather | solution.py:172
  17.6 10.0 copy-start.21
  17.6 302.0 %copy-start.22 = (bf16[1,2,34]{2,1,0:T(2,128)(2,1)S(1)}, bf16[1,2,34]{2,1,0:T(2,128)(2,1)}, u32[]{:S(2)}) copy-start(bf16[1,2,34]{2,1,0:T(2,128)(2,1)} %param.11) | copy-start | bytes 412
  17.6 408.1 %all-to-all-start = ((bf16[32,34,4352]{2,1,0:T(8,128)(2,1)}), bf16[32,34,4352]{2,1,0:T(8,128)(2,1)}, u32[]{:S(2)}, u32[]{:S(2)}) async-start(bf16[32,34,4352]{2,1,0:T(8,128)(2,1)} %stack.65), calls=%async_computation | async-start | bytes 22282240 | tf_op jit(solution)/shard_map/all_to_all | solution.py:159
  27.6 361.8 %copy-start = (bf16[128,1088]{0,1:T(8,128)(2,1)S(1)}, bf16[128,1088]{0,1:T(8,128)(2,1)}, u32[]{:S(2)}) copy-start(bf16[128,1088]{0,1:T(8,128)(2,1)} %param.9) | copy-start | bytes 835588
  27.6 362.1 %copy-start.15 = (s32[128]{0:T(128)S(1)}, s32[128]{0:T(128)}, u32[]{:S(2)}) copy-start(s32[128]{0:T(128)} %param.10) | copy-start | bytes 1540
  27.6 1242.0 %reduce-scatter.33.cloned.1.call-start = ((), (), s32[]{:S(2)}) async-start(), calls=%async_computation.13 | async-start | bytes 10340352
  389.7 46.9 %copy-start.19 = (f32[128]{0:T(128)}, f32[128]{0:T(128)S(1)}, u32[]{:S(2)}) copy-start(f32[128]{0:T(128)S(1)} %fusion.55) | copy-start | bytes 1540
  446.3 32.5 %copy-start.6 = (bf16[17,64,128]{2,1,0:T(8,128)(2,1)}, bf16[17,64,128]{2,1,0:T(8,128)(2,1)S(1)}, u32[]{:S(2)}) copy-start(bf16[17,64,128]{2,1,0:T(8,128)(2,1)S(1)} %convolution_convert_fusion.7) | copy-start | bytes 835588
  478.8 10.9 copy-start.5
  495.0 168.5 %slice-start = ((s8[9469952]{0:T(1024)(128)(4,1)}), s8[1081344]{0:T(1024)(128)(4,1)S(1)}, s32[]{:S(2)}) async-start(s8[9469952]{0:T(1024)(128)(4,1)} %bitcast.160), calls=%async_computation.14 | async-start | bytes 2162688
  495.1 778.7 %reduce-scatter.27.cloned.1.call-start = ((), (), s32[]{:S(2)}) async-start(), calls=%async_computation.10 | async-start | bytes 348160
  645.7 21.0 %slice-start.3 = ((s8[5013504]{0:T(1024)(128)(4,1)}), s8[4194304]{0:T(1024)(128)(4,1)S(1)}, s32[]{:S(2)}) async-start(s8[5013504]{0:T(1024)(128)(4,1)} %bitcast.192), calls=%async_computation.17 | async-start | bytes 8388608
  645.7 17.8 %slice-start.1 = ((s8[9469952]{0:T(1024)(128)(4,1)}), s8[4194304]{0:T(1024)(128)(4,1)S(1)}, s32[]{:S(2)}) async-start(s8[9469952]{0:T(1024)(128)(4,1)} %bitcast.160), calls=%async_computation.15 | async-start | bytes 8388608
  645.7 17.8 %slice-start.2 = ((s8[9469952]{0:T(1024)(128)(4,1)}), s8[4194304]{0:T(1024)(128)(4,1)S(1)}, s32[]{:S(2)}) async-start(s8[9469952]{0:T(1024)(128)(4,1)} %bitcast.160), calls=%async_computation.16 | async-start | bytes 8388608
  645.7 21.0 %slice-start.4 = ((s8[5013504]{0:T(1024)(128)(4,1)}), s8[819200]{0:T(1024)(128)(4,1)S(1)}, s32[]{:S(2)}) async-start(s8[5013504]{0:T(1024)(128)(4,1)} %bitcast.192), calls=%async_computation.18 | async-start | bytes 1638400
  1028.9 25.1 %collective-permute-start.13 = (bf16[48,1088]{1,0:T(8,128)(2,1)S(1)}, bf16[48,1088]{1,0:T(8,128)(2,1)S(1)}, u32[]{:S(2)}, u32[]{:S(2)}) collective-permute-start(bf16[48,1088]{1,0:T(8,128)(2,1)S(1)} %get-tuple-element.51), channel_id=1, source_target_pairs={{0,9},{1,10},{2,11},{3,12},{4,13},{5,14},{6,15},{7,16},{8,17},{9,1... | collective-permute-start | bytes 313352
  1030.2 25.7 %collective-permute-start.12 = (bf16[48,1088]{1,0:T(8,128)(2,1)S(1)}, bf16[48,1088]{1,0:T(8,128)(2,1)S(1)}, u32[]{:S(2)}, u32[]{:S(2)}) collective-permute-start(bf16[48,1088]{1,0:T(8,128)(2,1)S(1)} %get-tuple-element.51), channel_id=1, source_target_pairs={{0,8},{1,9},{2,10},{3,11},{4,12},{5,13},{6,14},{7,15},{8,16},{9,17... | collective-permute-start | bytes 313352
  1031.5 33.5 %collective-permute-start.11 = (bf16[48,1088]{1,0:T(8,128)(2,1)S(1)}, bf16[48,1088]{1,0:T(8,128)(2,1)S(1)}, u32[]{:S(2)}, u32[]{:S(2)}) collective-permute-start(bf16[48,1088]{1,0:T(8,128)(2,1)S(1)} %get-tuple-element.51), channel_id=1, source_target_pairs={{0,7},{1,8},{2,9},{3,10},{4,11},{5,12},{6,13},{7,14},{8,15},{9,16}... | collective-permute-start | bytes 313352
  1038.2 95.1 %collective-permute-start.10 = (bf16[48,1088]{1,0:T(8,128)(2,1)S(1)}, bf16[48,1088]{1,0:T(8,128)(2,1)}, u32[]{:S(2)}, u32[]{:S(2)}) collective-permute-start(bf16[48,1088]{1,0:T(8,128)(2,1)S(1)} %get-tuple-element.51), channel_id=1, source_target_pairs={{0,6},{1,7},{2,8},{3,9},{4,10},{5,11},{6,12},{7,13},{8,14},{9,15},... | collective-permute-start | bytes 313352
  1040.1 7.3 copy-start.20
  1047.4 150.4 %copy-start.8 = (f32[128,1088]{0,1:T(8,128)}, f32[128,1088]{0,1:T(8,128)S(1)}, u32[]{:S(2)}) copy-start(f32[128,1088]{0,1:T(8,128)S(1)} %get-tuple-element.64) | copy-start | bytes 1671172
  1047.9 2.0 collective-permute-start.14
  1049.9 84.7 %collective-permute-start.9 = (bf16[48,1088]{1,0:T(8,128)(2,1)S(1)}, bf16[48,1088]{1,0:T(8,128)(2,1)S(1)}, u32[]{:S(2)}, u32[]{:S(2)}) collective-permute-start(bf16[48,1088]{1,0:T(8,128)(2,1)S(1)} %get-tuple-element.51), channel_id=1, source_target_pairs={{0,5},{1,6},{2,7},{3,8},{4,9},{5,10},{6,11},{7,12},{8,13},{9,14},{... | collective-permute-start | bytes 313352
  1054.0 82.6 %collective-permute-start.8 = (bf16[48,1088]{1,0:T(8,128)(2,1)S(1)}, bf16[48,1088]{1,0:T(8,128)(2,1)S(1)}, u32[]{:S(2)}, u32[]{:S(2)}) collective-permute-start(bf16[48,1088]{1,0:T(8,128)(2,1)S(1)} %get-tuple-element.51), channel_id=1, source_target_pairs={{0,4},{1,5},{2,6},{3,7},{4,8},{5,9},{6,10},{7,11},{8,12},{9,13},{1... | collective-permute-start | bytes 313352
  1056.0 82.6 %collective-permute-start.7 = (bf16[48,1088]{1,0:T(8,128)(2,1)S(1)}, bf16[48,1088]{1,0:T(8,128)(2,1)S(1)}, u32[]{:S(2)}, u32[]{:S(2)}) collective-permute-start(bf16[48,1088]{1,0:T(8,128)(2,1)S(1)} %get-tuple-element.51), channel_id=1, source_target_pairs={{0,3},{1,4},{2,5},{3,6},{4,7},{5,8},{6,9},{7,10},{8,11},{9,12},{10... | collective-permute-start | bytes 313352
  1065.6 76.5 %collective-permute-start.6 = (bf16[48,1088]{1,0:T(8,128)(2,1)S(1)}, bf16[48,1088]{1,0:T(8,128)(2,1)S(1)}, u32[]{:S(2)}, u32[]{:S(2)}) collective-permute-start(bf16[48,1088]{1,0:T(8,128)(2,1)S(1)} %get-tuple-element.51), channel_id=1, source_target_pairs={{0,2},{1,3},{2,4},{3,5},{4,6},{5,7},{6,8},{7,9},{8,10},{9,11},{10,... | collective-permute-start | bytes 313352
  1133.3 66.0 %collective-permute-start.3 = (bf16[40,3264]{1,0:T(8,128)(2,1)S(1)}, bf16[40,3264]{1,0:T(8,128)(2,1)S(1)}, u32[]{:S(2)}, u32[]{:S(2)}) collective-permute-start(bf16[40,3264]{1,0:T(8,128)(2,1)S(1)} %get-tuple-element.50), channel_id=1, source_target_pairs={{0,4},{1,5},{2,6},{3,7},{4,8},{5,9},{6,10},{7,11},{8,12},{9,13},{1... | collective-permute-start | bytes 783368
  1134.6 66.9 %collective-permute-start.2 = (bf16[40,3264]{1,0:T(8,128)(2,1)S(1)}, bf16[40,3264]{1,0:T(8,128)(2,1)}, u32[]{:S(2)}, u32[]{:S(2)}) collective-permute-start(bf16[40,3264]{1,0:T(8,128)(2,1)S(1)} %get-tuple-element.50), channel_id=1, source_target_pairs={{0,3},{1,4},{2,5},{3,6},{4,7},{5,8},{6,9},{7,10},{8,11},{9,12},{10... | collective-permute-start | bytes 783368
  1136.6 7.5 copy-start.12
  1136.6 68.2 %collective-permute-start.1 = (bf16[40,3264]{1,0:T(8,128)(2,1)S(1)}, bf16[40,3264]{1,0:T(8,128)(2,1)}, u32[]{:S(2)}, u32[]{:S(2)}) collective-permute-start(bf16[40,3264]{1,0:T(8,128)(2,1)S(1)} %get-tuple-element.50), channel_id=1, source_target_pairs={{0,2},{1,3},{2,4},{3,5},{4,6},{5,7},{6,8},{7,9},{8,10},{9,11},{10,... | collective-permute-start | bytes 783368
  1138.6 39.7 %copy-start.13 = (bf16[48,1088]{1,0:T(8,128)(2,1)}, bf16[48,1088]{1,0:T(8,128)(2,1)S(1)}, u32[]{:S(2)}) copy-start(bf16[48,1088]{1,0:T(8,128)(2,1)S(1)} %collective-permute-done.7) | copy-start | bytes 313348
  1138.6 70.9 %collective-permute-start = (bf16[40,3264]{1,0:T(8,128)(2,1)S(1)}, bf16[40,3264]{1,0:T(8,128)(2,1)}, u32[]{:S(2)}, u32[]{:S(2)}) collective-permute-start(bf16[40,3264]{1,0:T(8,128)(2,1)S(1)} %get-tuple-element.50), channel_id=1, source_target_pairs={{0,1},{1,2},{2,3},{3,4},{4,5},{5,6},{6,7},{7,8},{8,9},{9,10},{10,1... | collective-permute-start | bytes 783368
  1142.1 36.2 %copy-start.14 = (bf16[48,1088]{1,0:T(8,128)(2,1)}, bf16[48,1088]{1,0:T(8,128)(2,1)S(1)}, u32[]{:S(2)}) copy-start(bf16[48,1088]{1,0:T(8,128)(2,1)S(1)} %collective-permute-done.6) | copy-start | bytes 313348
  1142.2 36.2 %collective-permute-start.5 = (bf16[48,1088]{1,0:T(8,128)(2,1)S(1)}, bf16[48,1088]{1,0:T(8,128)(2,1)}, u32[]{:S(2)}, u32[]{:S(2)}) collective-permute-start(bf16[48,1088]{1,0:T(8,128)(2,1)S(1)} %get-tuple-element.51), channel_id=1, source_target_pairs={{0,1},{1,2},{2,3},{3,4},{4,5},{5,6},{6,7},{7,8},{8,9},{9,10},{10,1... | collective-permute-start | bytes 313352
  1178.4 19.5 %collective-permute-start.4 = (bf16[26,3264]{1,0:T(8,128)(2,1)S(1)}, bf16[26,3264]{1,0:T(8,128)(2,1)S(1)}, u32[]{:S(2)}, u32[]{:S(2)}) collective-permute-start(bf16[26,3264]{1,0:T(8,128)(2,1)S(1)} %slice.44), channel_id=1, source_target_pairs={{0,5},{1,6},{2,7},{3,8},{4,9},{5,10},{6,11},{7,12},{8,13},{9,14},{... | collective-permute-start | bytes 509192
  1197.8 87.7 %reduce-scatter.25.cloned.1.call-start = ((), (), s32[]{:S(2)}) async-start(), calls=%async_computation.9 | async-start | bytes 1044480
  1197.9 39.1 %collective-permute-start.18 = (bf16[40,4352]{1,0:T(8,128)(2,1)S(1)}, bf16[40,4352]{1,0:T(8,128)(2,1)S(1)}, u32[]{:S(2)}, u32[]{:S(2)}) collective-permute-start(bf16[40,4352]{1,0:T(8,128)(2,1)S(1)} %get-tuple-element.52), channel_id=1, source_target_pairs={{0,4},{1,5},{2,6},{3,7},{4,8},{5,9},{6,10},{7,11},{8,12},{9,13},{1... | collective-permute-start | bytes 1044488
  1199.2 37.7 %collective-permute-start.17 = (bf16[40,4352]{1,0:T(8,128)(2,1)S(1)}, bf16[40,4352]{1,0:T(8,128)(2,1)S(1)}, u32[]{:S(2)}, u32[]{:S(2)}) collective-permute-start(bf16[40,4352]{1,0:T(8,128)(2,1)S(1)} %get-tuple-element.52), channel_id=1, source_target_pairs={{0,3},{1,4},{2,5},{3,6},{4,7},{5,8},{6,9},{7,10},{8,11},{9,12},{10... | collective-permute-start | bytes 1044488
  1201.5 35.5 %collective-permute-start.16 = (bf16[40,4352]{1,0:T(8,128)(2,1)S(1)}, bf16[40,4352]{1,0:T(8,128)(2,1)}, u32[]{:S(2)}, u32[]{:S(2)}) collective-permute-start(bf16[40,4352]{1,0:T(8,128)(2,1)S(1)} %get-tuple-element.52), channel_id=1, source_target_pairs={{0,2},{1,3},{2,4},{3,5},{4,6},{5,7},{6,8},{7,9},{8,10},{9,11},{10,... | collective-permute-start | bytes 1044488
  1204.8 32.2 %collective-permute-start.15 = (bf16[40,4352]{1,0:T(8,128)(2,1)S(1)}, bf16[40,4352]{1,0:T(8,128)(2,1)}, u32[]{:S(2)}, u32[]{:S(2)}) collective-permute-start(bf16[40,4352]{1,0:T(8,128)(2,1)S(1)} %get-tuple-element.52), channel_id=1, source_target_pairs={{0,1},{1,2},{2,3},{3,4},{4,5},{5,6},{6,7},{7,8},{8,9},{9,10},{10,1... | collective-permute-start | bytes 1044488
  1209.5 27.4 %collective-permute-start.19 = (bf16[26,4352]{1,0:T(8,128)(2,1)}, bf16[26,4352]{1,0:T(8,128)(2,1)}, u32[]{:S(2)}, u32[]{:S(2)}) collective-permute-start(bf16[26,4352]{1,0:T(8,128)(2,1)} %slice.46), channel_id=1, source_target_pairs={{0,5},{1,6},{2,7},{3,8},{4,9},{5,10},{6,11},{7,12},{8,13},{9,14},{... | collective-permute-start | bytes 678920
  1236.9 64.6 %reduce-scatter.29.cloned.1.call-start = ((), (), s32[]{:S(2)}) async-start(), calls=%async_computation.11 | async-start | bytes 1392640
  1261.9 9.7 copy-start.4
  1261.9 9.7 copy-start.18
  1262.0 71.0 %reduce-scatter.31.cloned.1.call-start = ((), (), s32[]{:S(2)}) async-start(), calls=%async_computation.12 | async-start | bytes 696320
  (9 other events, 10.3 us)
Sparse Core Ops, SparseCore 0:
  10.2 319.9 all-gather.12
  332.4 142.6 all-gather.14
  476.8 168.8 all-gather.16
  648.0 233.4 reduce-scatter.32
  1198.0 34.4 reduce-scatter.26
  1237.0 30.2 reduce-scatter.24
  1270.0 31.5 reduce-scatter.28
  1304.7 28.1 reduce-scatter.30
